TPU v7x, 32 devices: a whole 2x2x4 slice. The times are simulated.
32 devices in a mesh: seq: 2 (over x), fsdp: 16 (over z, y, core).
Axes of the slice: x: 2, y: 2, z: 4, core: 2. Of those that a mesh axis runs over, the one named last changes fastest.
Arguments:
- tokens: bfloat16 [16, 1024, 768], P('fsdp', 'seq'), may hold values from -6 to 6
- prior_logits: bfloat16 [16, 12, 1024, 1024], P('fsdp', 'seq'), may hold values from -6 to 6
- lengths: int32 [16], P('fsdp'), may hold values from 256 to 1024, as said below
- order: int32 [16, 1024], P('fsdp'), may hold values from 0 to 1023, each once within a row
- cotangent: bfloat16 [16, 1024, 768], P('fsdp', 'seq'), may hold values from -6 to 6
- w_qkv: bfloat16 [768, 2304], P('fsdp'), may hold values from -0.21875 to 0.21875
- w_out: bfloat16 [768, 768], P('fsdp'), may hold values from -3.5 to 3.5
- w_in: bfloat16 [768, 3072], P('fsdp'), may hold values from -0.21875 to 0.21875
- w_back: bfloat16 [3072, 768], P('fsdp'), may hold values from -0.109375 to 0.109375
- bias_q: bfloat16 [768], P('fsdp'), may hold values from -1.5 to 1.5
- bias_v: bfloat16 [768], P('fsdp'), may hold values from -0.25 to 0.25
- bias_o: bfloat16 [768], P('fsdp'), may hold values from -1.5 to 1.5
- gain_one: bfloat16 [768], P('fsdp'), may hold values from 0.5 to 1.5
- shift_one: bfloat16 [768], P('fsdp'), may hold values from -1.5 to 1.5
- bias_in: bfloat16 [3072], P('fsdp'), may hold values from -1.5 to 1.5
- bias_back: bfloat16 [768], P('fsdp'), may hold values from -1.5 to 1.5
- gain_two: bfloat16 [768], P('fsdp'), may hold values from 0.5 to 1.5
- shift_two: bfloat16 [768], P('fsdp'), may hold values from -1.5 to 1.5
Outputs:
- output: bfloat16 [16, 1024, 768], P('fsdp', 'seq')
- raw_logits: bfloat16 [16, 12, 1024, 1024], P('fsdp', 'seq')
- tokens_grad: bfloat16 [16, 1024, 768], P('fsdp', 'seq')
- prior_grad: bfloat16 [16, 12, 1024, 1024], P('fsdp', 'seq')
- grad_w_qkv: float32 [768, 2304], P('fsdp')
- grad_w_out: float32 [768, 768], P('fsdp')
- grad_w_in: float32 [768, 3072], P('fsdp')
- grad_w_back: float32 [3072, 768], P('fsdp')
- grad_bias_q: float32 [768], P('fsdp')
- grad_bias_v: float32 [768], P('fsdp')
- grad_bias_o: float32 [768], P('fsdp')
- grad_gain_one: float32 [768], P('fsdp')
- grad_shift_one: float32 [768], P('fsdp')
- grad_bias_in: float32 [3072], P('fsdp')
- grad_bias_back: float32 [768], P('fsdp')
- grad_gain_two: float32 [768], P('fsdp')
- grad_shift_two: float32 [768], P('fsdp')
- rms: float32 [3], replicated
Inputs may be any that keep to these rules, and one draw needn't show every extreme that they name: `lengths`: positions below a sequence's length hold its tokens, the others are padding; some sequence has exactly 1024.
All inputs are finite; a program needn't handle non-finite values.
Results may differ from a plain program's by a relative error of at most 0.017.
Values may be sent and summed in bfloat16 or wider, within the bound.
No kernel may reach another device: no remote copies, remote signals or barrier semaphores. Data moves between devices by JAX's collectives and lax.ppermute only.
A program may use at most 192 MiB of HBM per device.

v0:
```python
import math
import jax
import jax.numpy as jnp
from jax import lax
from jax.sharding import PartitionSpec as P

HD = 64
eps_norm = 1e-05
masked_fill = -1e30


def layer_norm(values, gain, shift):
    average = jnp.mean(values, axis=-1, keepdims=True)
    centered = values - average
    variance = jnp.mean(centered * centered, axis=-1, keepdims=True)
    return centered * lax.rsqrt(variance + eps_norm) * gain + shift


def gelu_exact(values):
    return jax.nn.gelu(values, approximate=False)


def contract_rows(left, right):
    return lax.dot_general(
        left, right, (((0,), (0,)), ((), ())), preferred_element_type=jnp.float32
    )


def contract_cols(left, right):
    return lax.dot_general(
        left, right, (((1,), (1,)), ((), ())), preferred_element_type=jnp.float32
    )


def body(
    tokens,
    prior_logits,
    lengths,
    order,
    cotangent,
    w_qkv,
    w_out,
    w_in,
    w_back,
    bias_q,
    bias_v,
    bias_o,
    gain_one,
    shift_one,
    bias_in,
    bias_back,
    gain_two,
    shift_two,
):
    seq_count = lax.axis_size("seq")
    seq_index = lax.axis_index("seq")
    qkv_weight, proj_weight, query_bias, value_bias, proj_bias, first_gain, first_shift = (
        lax.all_gather(w_qkv, "fsdp", axis=0, tiled=True),
        lax.all_gather(w_out, "fsdp", axis=0, tiled=True),
        lax.all_gather(bias_q, "fsdp", axis=0, tiled=True),
        lax.all_gather(bias_v, "fsdp", axis=0, tiled=True),
        lax.all_gather(bias_o, "fsdp", axis=0, tiled=True),
        lax.all_gather(gain_one, "fsdp", axis=0, tiled=True),
        lax.all_gather(shift_one, "fsdp", axis=0, tiled=True),
    )
    rows = tokens[0]
    local_count = rows.shape[0]
    width = rows.shape[1]
    heads_local = prior_logits.shape[1]
    local_width = heads_local * HD
    total = local_count * seq_count
    scale = 1.0 / math.sqrt(HD)
    joint_bias = jnp.concatenate(
        [
            query_bias.astype(jnp.float32),
            jnp.zeros((width,), jnp.float32),
            value_bias.astype(jnp.float32),
        ]
    )
    joint = (jnp.dot(rows, qkv_weight, preferred_element_type=jnp.float32) + joint_bias).astype(
        jnp.bfloat16
    )
    joint = joint.reshape(local_count, 3, seq_count, local_width)
    headed = lax.all_to_all(joint, "seq", split_axis=2, concat_axis=0, tiled=True).reshape(
        total, 3, local_width
    )
    order_row = order[0]
    length = lengths[0]
    positions = jnp.arange(total, dtype=jnp.int32)
    inverse = jnp.zeros((total,), jnp.int32).at[order_row].set(positions)
    placed = headed[inverse]
    query_pos = placed[:, 0].reshape(total, heads_local, HD)
    key_pos = placed[:, 1].reshape(total, heads_local, HD)
    value_pos = placed[:, 2].reshape(total, heads_local, HD)
    key_valid = (positions < length)[None, None, :]
    prior = prior_logits[0]
    block = min(512, total)
    block_count = total // block

    def block_scores(start):
        query_blk = lax.dynamic_slice_in_dim(query_pos, start, block, 0)
        prior_blk = lax.dynamic_slice_in_dim(prior, start, block, 1).astype(jnp.float32)
        scores = (
            jnp.einsum("qhd,khd->hqk", query_blk, key_pos, preferred_element_type=jnp.float32)
            * scale
            + prior_blk
        )
        return (query_blk, scores)

    def forward_block(block_index, carry):
        raw_buf, context_buf, lse_buf = carry
        start = block_index * block
        query_blk, scores = block_scores(start)
        masked = jnp.where(key_valid, scores, masked_fill)
        largest = jnp.max(masked, axis=-1, keepdims=True)
        exponent = jnp.exp(masked - largest)
        row_total = jnp.sum(exponent, axis=-1, keepdims=True)
        weights = (exponent / row_total).astype(jnp.bfloat16)
        context_blk = jnp.einsum(
            "hqk,khd->qhd", weights, value_pos, preferred_element_type=jnp.float32
        ).astype(jnp.bfloat16)
        raw_buf = lax.dynamic_update_slice_in_dim(raw_buf, scores.astype(jnp.bfloat16), start, 1)
        context_buf = lax.dynamic_update_slice_in_dim(context_buf, context_blk, start, 0)
        lse_buf = lax.dynamic_update_slice_in_dim(lse_buf, largest + jnp.log(row_total), start, 1)
        return (raw_buf, context_buf, lse_buf)

    raw_buf, context_pos, lse_buf = lax.fori_loop(
        0,
        block_count,
        forward_block,
        (
            jnp.zeros((heads_local, total, total), jnp.bfloat16),
            jnp.zeros((total, heads_local, HD), jnp.bfloat16),
            jnp.zeros((heads_local, total, 1), jnp.float32),
        ),
    )
    context_stored = context_pos.reshape(total, local_width)[order_row].reshape(
        total, 1, local_width
    )
    context = lax.all_to_all(
        context_stored, "seq", split_axis=0, concat_axis=1, tiled=True
    ).reshape(local_count, width)
    attended = jnp.dot(context, proj_weight, preferred_element_type=jnp.float32) + proj_bias.astype(
        jnp.float32
    )
    tokens_f = rows.astype(jnp.float32)
    residual_one = tokens_f + attended
    hidden, norm_back_one = jax.vjp(
        layer_norm, residual_one, first_gain.astype(jnp.float32), first_shift.astype(jnp.float32)
    )
    hidden_low = hidden.astype(jnp.bfloat16)
    inner_weight, outer_weight, inner_bias, outer_bias, second_gain, second_shift = (
        lax.all_gather(w_in, "fsdp", axis=0, tiled=True),
        lax.all_gather(w_back, "fsdp", axis=0, tiled=True),
        lax.all_gather(bias_in, "fsdp", axis=0, tiled=True),
        lax.all_gather(bias_back, "fsdp", axis=0, tiled=True),
        lax.all_gather(gain_two, "fsdp", axis=0, tiled=True),
        lax.all_gather(shift_two, "fsdp", axis=0, tiled=True),
    )
    inner = jnp.dot(
        hidden_low, inner_weight, preferred_element_type=jnp.float32
    ) + inner_bias.astype(jnp.float32)
    activated_f, gelu_back = jax.vjp(gelu_exact, inner)
    activated = activated_f.astype(jnp.bfloat16)
    branch = jnp.dot(
        activated, outer_weight, preferred_element_type=jnp.float32
    ) + outer_bias.astype(jnp.float32)
    residual_two = hidden + branch
    normed_two, norm_back_two = jax.vjp(
        layer_norm, residual_two, second_gain.astype(jnp.float32), second_shift.astype(jnp.float32)
    )
    local_order = lax.dynamic_slice_in_dim(order_row, seq_index * local_count, local_count)
    valid_rows = (local_order < length).astype(jnp.float32)[:, None]
    sum_tokens, sum_attended, sum_branch, token_count = lax.psum(
        (
            jnp.sum(valid_rows * tokens_f * tokens_f),
            jnp.sum(valid_rows * attended * attended),
            jnp.sum(valid_rows * branch * branch),
            jnp.sum(valid_rows),
        ),
        ("seq", "fsdp"),
    )
    rms = jnp.sqrt(jnp.stack([sum_tokens, sum_attended, sum_branch]) / (token_count * width))
    d_output = cotangent[0].astype(jnp.float32) * valid_rows
    d_res_two, grad_gain_two, grad_shift_two = norm_back_two(d_output)
    d_branch = d_res_two.astype(jnp.bfloat16)
    grad_bias_back = jnp.sum(d_branch.astype(jnp.float32), axis=0)
    grad_w_back = contract_rows(activated, d_branch)
    d_activated = contract_cols(d_branch, outer_weight)
    d_inner = gelu_back(d_activated)[0].astype(jnp.bfloat16)
    grad_bias_in = jnp.sum(d_inner.astype(jnp.float32), axis=0)
    grad_w_in = contract_rows(hidden_low, d_inner)
    d_hidden = d_res_two + contract_cols(d_inner, inner_weight)
    d_res_one, grad_gain_one, grad_shift_one = norm_back_one(d_hidden)
    d_attended = d_res_one.astype(jnp.bfloat16)
    grad_bias_o = jnp.sum(d_attended.astype(jnp.float32), axis=0)
    grad_w_out = contract_rows(context, d_attended)
    d_context = contract_cols(d_attended, proj_weight).astype(jnp.bfloat16)
    d_context = d_context.reshape(local_count, seq_count, local_width)
    d_context_all = lax.all_to_all(
        d_context, "seq", split_axis=1, concat_axis=0, tiled=True
    ).reshape(total, local_width)
    d_context_pos = d_context_all[inverse].reshape(total, heads_local, HD)

    def backward_block(block_index, carry):
        dprior_buf, dquery_buf, dkey_acc, dvalue_acc = carry
        start = block_index * block
        query_blk, scores = block_scores(start)
        masked = jnp.where(key_valid, scores, masked_fill)
        lse_blk = lax.dynamic_slice_in_dim(lse_buf, start, block, 1)
        probability = jnp.exp(masked - lse_blk)
        weights = probability.astype(jnp.bfloat16)
        dcontext_blk = lax.dynamic_slice_in_dim(d_context_pos, start, block, 0)
        d_prob = jnp.einsum(
            "qhd,khd->hqk", dcontext_blk, value_pos, preferred_element_type=jnp.float32
        )
        row_term = jnp.sum(probability * d_prob, axis=-1, keepdims=True)
        d_scores = (probability * (d_prob - row_term)).astype(jnp.bfloat16)
        dprior_buf = lax.dynamic_update_slice_in_dim(dprior_buf, d_scores, start, 1)
        dquery_blk = (
            jnp.einsum("hqk,khd->qhd", d_scores, key_pos, preferred_element_type=jnp.float32)
            * scale
        )
        dquery_buf = lax.dynamic_update_slice_in_dim(dquery_buf, dquery_blk, start, 0)
        dkey_acc = (
            dkey_acc
            + jnp.einsum("hqk,qhd->khd", d_scores, query_blk, preferred_element_type=jnp.float32)
            * scale
        )
        dvalue_acc = dvalue_acc + jnp.einsum(
            "hqk,qhd->khd", weights, dcontext_blk, preferred_element_type=jnp.float32
        )
        return (dprior_buf, dquery_buf, dkey_acc, dvalue_acc)

    dprior_buf, dquery_buf, dkey_acc, dvalue_acc = lax.fori_loop(
        0,
        block_count,
        backward_block,
        (
            jnp.zeros((heads_local, total, total), jnp.bfloat16),
            jnp.zeros((total, heads_local, HD), jnp.float32),
            jnp.zeros((total, heads_local, HD), jnp.float32),
            jnp.zeros((total, heads_local, HD), jnp.float32),
        ),
    )
    d_joint_pos = jnp.stack(
        [
            dquery_buf.reshape(total, local_width),
            dkey_acc.reshape(total, local_width),
            dvalue_acc.reshape(total, local_width),
        ],
        axis=1,
    ).astype(jnp.bfloat16)
    d_joint_stored = d_joint_pos[order_row].reshape(total, 3, 1, local_width)
    d_joint = lax.all_to_all(
        d_joint_stored, "seq", split_axis=0, concat_axis=2, tiled=True
    ).reshape(local_count, 3 * width)
    grad_bias_q = jnp.sum(d_joint[:, :width].astype(jnp.float32), axis=0)
    grad_bias_v = jnp.sum(d_joint[:, 2 * width :].astype(jnp.float32), axis=0)
    grad_w_qkv = contract_rows(rows, d_joint)
    tokens_grad = (d_res_one + contract_cols(d_joint, qkv_weight)).astype(jnp.bfloat16)
    (
        pair_qkv,
        pair_out,
        pair_in,
        pair_back,
        pair_bias_q,
        pair_bias_v,
        pair_bias_o,
        pair_gain_one,
        pair_shift_one,
        pair_bias_in,
        pair_bias_back,
        pair_gain_two,
        pair_shift_two,
    ) = (
        lax.psum(grad_w_qkv.astype(jnp.bfloat16), "seq").astype(jnp.float32),
        lax.psum(grad_w_out.astype(jnp.bfloat16), "seq").astype(jnp.float32),
        lax.psum(grad_w_in.astype(jnp.bfloat16), "seq").astype(jnp.float32),
        lax.psum(grad_w_back.astype(jnp.bfloat16), "seq").astype(jnp.float32),
        lax.psum(grad_bias_q.astype(jnp.bfloat16), "seq").astype(jnp.float32),
        lax.psum(grad_bias_v.astype(jnp.bfloat16), "seq").astype(jnp.float32),
        lax.psum(grad_bias_o.astype(jnp.bfloat16), "seq").astype(jnp.float32),
        lax.psum(grad_gain_one.astype(jnp.bfloat16), "seq").astype(jnp.float32),
        lax.psum(grad_shift_one.astype(jnp.bfloat16), "seq").astype(jnp.float32),
        lax.psum(grad_bias_in.astype(jnp.bfloat16), "seq").astype(jnp.float32),
        lax.psum(grad_bias_back.astype(jnp.bfloat16), "seq").astype(jnp.float32),
        lax.psum(grad_gain_two.astype(jnp.bfloat16), "seq").astype(jnp.float32),
        lax.psum(grad_shift_two.astype(jnp.bfloat16), "seq").astype(jnp.float32),
    )
    owned = (
        lax.psum_scatter(pair_qkv, "fsdp", scatter_dimension=0, tiled=True),
        lax.psum_scatter(pair_out, "fsdp", scatter_dimension=0, tiled=True),
        lax.psum_scatter(pair_in, "fsdp", scatter_dimension=0, tiled=True),
        lax.psum_scatter(pair_back, "fsdp", scatter_dimension=0, tiled=True),
        lax.psum_scatter(pair_bias_q, "fsdp", scatter_dimension=0, tiled=True),
        lax.psum_scatter(pair_bias_v, "fsdp", scatter_dimension=0, tiled=True),
        lax.psum_scatter(pair_bias_o, "fsdp", scatter_dimension=0, tiled=True),
        lax.psum_scatter(pair_gain_one, "fsdp", scatter_dimension=0, tiled=True),
        lax.psum_scatter(pair_shift_one, "fsdp", scatter_dimension=0, tiled=True),
        lax.psum_scatter(pair_bias_in, "fsdp", scatter_dimension=0, tiled=True),
        lax.psum_scatter(pair_bias_back, "fsdp", scatter_dimension=0, tiled=True),
        lax.psum_scatter(pair_gain_two, "fsdp", scatter_dimension=0, tiled=True),
        lax.psum_scatter(pair_shift_two, "fsdp", scatter_dimension=0, tiled=True),
    )
    return (
        normed_two.astype(jnp.bfloat16)[None],
        raw_buf[None],
        tokens_grad[None],
        dprior_buf[None],
        owned[0],
        owned[1],
        owned[2],
        owned[3],
        owned[4],
        owned[5],
        owned[6],
        owned[7],
        owned[8],
        owned[9],
        owned[10],
        owned[11],
        owned[12],
        rms,
    )


def solution(mesh):
    return jax.shard_map(
        body,
        mesh=mesh,
        in_specs=(
            P("fsdp", "seq", None),
            P("fsdp", "seq", None, None),
            P("fsdp"),
            P("fsdp", None),
            P("fsdp", "seq", None),
            P("fsdp", None),
            P("fsdp", None),
            P("fsdp", None),
            P("fsdp", None),
            P("fsdp"),
            P("fsdp"),
            P("fsdp"),
            P("fsdp"),
            P("fsdp"),
            P("fsdp"),
            P("fsdp"),
            P("fsdp"),
            P("fsdp"),
        ),
        out_specs=(
            P("fsdp", "seq", None),
            P("fsdp", "seq", None, None),
            P("fsdp", "seq", None),
            P("fsdp", "seq", None, None),
            P("fsdp", None),
            P("fsdp", None),
            P("fsdp", None),
            P("fsdp", None),
            P("fsdp"),
            P("fsdp"),
            P("fsdp"),
            P("fsdp"),
            P("fsdp"),
            P("fsdp"),
            P("fsdp"),
            P("fsdp"),
            P("fsdp"),
            P(),
        ),
        check_vma=False,
    )
```

profile of v0, /device:TPU:0, one launch (start us, length us, event | category | flops | bytes accessed | tf_op | source)
XLA Modules:
  0.0 1158.4 jit_solution(11270746098248359767)
XLA Ops:
  19.6 63.9 %all-reduce.20 = (bf16[768]{0:T(1024)(128)(2,1)S(1)}, bf16[768]{0:T(1024)(128)(2,1)S(1)}, bf16[768]{0:T(1024)(128)(2,1)}, bf16[768]{0:T(1024)(128)(2,1)}, bf16[7...) all-reduce(bf16[768]{0:T(1024)(128)(2,1)S(1)} %dynamic-update-slice, ...), channel_id=1, replica_groups=mesh['seq'=2,'fsdp'=16] {'fsdp'}, use_global_device_ids=true, to_apply=%add.1 | all-reduce | flops 9216 | bytes 36864
  105.4 17.6 %all-to-all-done = bf16[512,3,2,384]{3,0,1,2:T(8,128)(2,1)S(1)} async-done(((bf16[512,3,2,384]{3,0,1,2:T(8,128)(2,1)}), bf16[512,3,2,384]{3,0,1,2:T(8,128)(2,1)S(1)}, u32[]{:S(2)}, u32[]{:S(2)}) %all-to-all-start) | async-done | bytes 2359328 | tf_op jit(solution)/shard_map/all_to_all | solution.py:84
  155.7 31.1 %while.38 = (s32[]{:T(128)}, bf16[6,1024,1024]{2,1,0:T(8,128)(2,1)}, bf16[1024,6,64]{0,2,1:T(8,128)(2,1)S(1)}, f32[6,1024,1]{1,0,2:T(8,128)S(1)}, bf16[1024,6,64...) while((s32[]{:T(128)}, ...), condition=%wide.region_4.5_spmd.clone, body=%wide.region_1.4_spmd.clone.sunk | while | flops 846395392 | bytes 65397944 | solution.py:127
  156.4 7.3 convert_dynamic-update-slice_fusion.2
  171.9 7.4 convert_dynamic-update-slice_fusion.2
  216.4 19.9 %multiply_convert_fusion.1 = (bf16[512,3072]{1,0:T(8,128)(2,1)}, f32[512,3072]{1,0:T(8,128)}, f32[512,3072]{1,0:T(8,128)}) fusion(f32[3072]{0:T(1024)S(1)} %convert_element_type.217, bf16[768,3072]{1,0:T(8,128)(2,1)} %all-gather.9.cloned.1.call-done, f32[512,768]{1,0:T(8,128)S(1)} %get-tuple-element.679, f32[768]{0:T(1024)S(1)} %convert_element_type.215, ...), kind=kOutput, calls=%fused_computation.47 | convolution fusion | flops 2521694208 | bytes 22042624 | tf_op jit(solution)/shard_map/dot_general | solution.py:160
  247.7 8.6 fusion.61
  267.0 7.9 all-to-all-done.2
  289.8 65.8 %while.39 = (s32[]{:T(128)}, bf16[6,1024,1024]{2,1,0:T(8,128)(2,1)}, bf16[1024,6,64]{0,2,1:T(8,128)(2,1)}, f32[1024,6,64]{0,2,1:T(8,128)S(1)}, f32[1024,6,64]{0,...) while((s32[]{:T(128)}, ...), condition=%wide.region_15.16_spmd.clone, body=%wide.region_13.0_spmd.clone.sunk | while | flops 2050029568 | bytes 127470920 | solution.py:235
  293.6 9.4 multiply_reduce_fusion.6
  310.0 8.9 constant_dynamic-update-slice_fusion.2
  326.3 9.5 multiply_reduce_fusion.6
  335.8 7.4 bitcast_add_fusion.5
  343.2 8.9 constant_dynamic-update-slice_fusion.2
  373.0 10.2 gather_fusion.3
  402.5 13.4 %all-to-all-done.3 = bf16[1024,3,1,384]{3,1,2,0:T(4,128)(2,1)S(1)} async-done(((bf16[1024,3,1,384]{3,1,2,0:T(4,128)(2,1)}), bf16[1024,3,1,384]{3,1,2,0:T(4,128)(2,1)S(1)}, u32[]{:S(2)}, u32[]{:S(2)}) %all-to-all-start.3) | async-done | bytes 2359328 | tf_op jit(solution)/shard_map/all_to_all | solution.py:255
  424.3 334.0 %all-reduce.25.cloned.1.call-done = (bf16[768,2304]{0,1:T(8,128)(2,1)}, bf16[768,768]{1,0:T(8,128)(2,1)}, bf16[768,3072]{1,0:T(8,128)(2,1)}, bf16[3072,768]{1,0:T(8,128)(2,1)}) async-done(((bf16[768,2304]{0,1:T(8,128)(2,1)}, bf16[768,768]{1,0:T(8,128)(2,1)}, bf16[768,3072]{1,0:T(8,128)(2,1)}, bf16[3072,768]{1,0:T(8,128)(2,1)}), (bf16[768,2304]{0,1:T(8,128)(2,1)}, bf16[768,768]{1,0:T(8,128)(2,1)}, ...) | async-done | bytes 14155792 | tf_op jit(solution)/shard_map/psum | solution.py:277
  767.3 7.3 convert_element_type.238
  782.9 40.3 %all-reduce.18 = (f32[1]{0:T(128)}, f32[1]{0:T(128)}, f32[1]{0:T(128)}, f32[]{:T(128)}) all-reduce(f32[1]{0:T(128)} %bitcast.38, f32[1]{0:T(128)} %bitcast.37, f32[1]{0:T(128)} %bitcast.36, f32[]{:T(128)} %get-tuple-element.662), channel_id=1, replica_groups=mesh['seq'=2,'fsdp'=16] {'seq','fsdp'}, use_global_device_ids=true, to_apply=%region_56.57 | all-reduce | flops 4 | bytes 32 | tf_op jit(solution)/shard_map/psum | solution.py:174
  826.7 9.1 all-reduce.21
  835.8 59.7 %all-reduce.19 = (f32[768]{0:T(1024)S(1)}, f32[768]{0:T(1024)S(1)}, f32[768]{0:T(1024)S(1)}, f32[768]{0:T(1024)S(1)}, f32[768]{0:T(1024)S(1)}, /*index=5*/f32[30...) all-reduce(bf16[768]{0:T(1024)(128)(2,1)S(1)} %get-tuple-element.64, ...), channel_id=6, replica_groups=mesh['seq'=2,'fsdp'=16] {'fsdp'}, use_global_device_ids=true, to_apply=%region_26.27.clone | all-reduce | flops 9216 | bytes 55296
  906.5 13.9 %reduce-scatter.13.cloned.1.call-done = f32[48,2304]{1,0:T(8,128)} async-done(((f32[768,2304]{1,0:T(8,128)}), f32[48,2304]{1,0:T(8,128)}) %reduce-scatter.13.cloned.1.call-update) | async-done | bytes 442384
  920.4 115.6 %reduce-scatter.9.cloned.1.call-done = f32[48,3072]{1,0:T(8,128)} async-done(((f32[768,3072]{1,0:T(8,128)}), f32[48,3072]{1,0:T(8,128)}) %reduce-scatter.9.cloned.1.call-update) | async-done | bytes 589840 | tf_op jit(solution)/shard_map/reduce_scatter | solution.py:294
  1036.0 115.5 %reduce-scatter.11.cloned.1.call-done = f32[192,768]{1,0:T(8,128)} async-done(((f32[3072,768]{1,0:T(8,128)}), f32[192,768]{1,0:T(8,128)}) %reduce-scatter.11.cloned.1.call-update) | async-done | bytes 589840 | tf_op jit(solution)/shard_map/reduce_scatter | solution.py:295
  (273 shorter events, 243.4 us)
Async XLA Ops:
  7.2 76.4 %all-gather.5.cloned.1.call-start = ((), (), s32[]{:S(2)}) async-start(), calls=%async_computation.8 | async-start | bytes 3760128 | tf_op jit(solution)/shard_map/all_gather | solution.py:58
  7.9 204.6 %all-gather.7.cloned.1.call-start = ((), (), s32[]{:S(2)}) async-start(), calls=%async_computation.9 | async-start | bytes 1253376 | tf_op jit(solution)/shard_map/all_gather | solution.py:59
  8.7 207.7 %all-gather.9.cloned.1.call-start = ((), (), s32[]{:S(2)}) async-start(), calls=%async_computation.10 | async-start | bytes 5013504 | tf_op jit(solution)/shard_map/all_gather | solution.py:153
  95.7 27.3 %all-to-all-start = ((bf16[512,3,2,384]{3,0,1,2:T(8,128)(2,1)}), bf16[512,3,2,384]{3,0,1,2:T(8,128)(2,1)S(1)}, u32[]{:S(2)}, u32[]{:S(2)}) async-start(bf16[512,3,2,384]{3,0,1,2:T(8,128)(2,1)} %copy.86), calls=%async_computation | async-start | bytes 4718592 | tf_op jit(solution)/shard_map/all_to_all | solution.py:84
  99.6 136.6 %all-gather.11.cloned.1.call-start = ((), (), s32[]{:S(2)}) async-start(), calls=%async_computation.11 | async-start | bytes 5013504 | tf_op jit(solution)/shard_map/all_gather | solution.py:154
  194.7 12.8 %all-to-all-start.1 = ((bf16[2,2,98304]{2,1,0:T(2,128)(2,1)}), bf16[2,2,98304]{2,1,0:T(2,128)(2,1)}, u32[]{:S(2)}, u32[]{:S(2)}) async-start(bf16[2,2,98304]{2,1,0:T(2,128)(2,1)} %reshape.336), calls=%async_computation.1 | async-start | bytes 1572864 | tf_op jit(solution)/shard_map/all_to_all | solution.py:140
  200.2 59.8 %copy-start.23 = (f32[768]{0:T(1024)}, f32[768]{0:T(1024)S(1)}, u32[]{:S(2)}) copy-start(f32[768]{0:T(1024)S(1)} %convert_element_type.214) | copy-start | bytes 9220
  216.0 44.0 %copy-start.4 = (f32[512,768]{1,0:T(8,128)}, f32[512,768]{1,0:T(8,128)S(1)}, u32[]{:S(2)}) copy-start(f32[512,768]{1,0:T(8,128)S(1)} %get-tuple-element.679) | copy-start | bytes 4718596
  216.0 44.0 %copy-start.21 = (f32[512]{0:T(512)}, f32[512]{0:T(512)S(1)}, u32[]{:S(2)}) copy-start(f32[512]{0:T(512)S(1)} %broadcast_multiply_fusion.1) | copy-start | bytes 6148
  263.5 11.5 all-to-all-start.2
  383.2 32.6 %all-to-all-start.3 = ((bf16[1024,3,1,384]{3,1,2,0:T(4,128)(2,1)}), bf16[1024,3,1,384]{3,1,2,0:T(4,128)(2,1)S(1)}, u32[]{:S(2)}, u32[]{:S(2)}) async-start(bf16[1024,3,1,384]{3,1,2,0:T(4,128)(2,1)} %bitcast.149), calls=%async_computation.3 | async-start | bytes 6291456 | tf_op jit(solution)/shard_map/all_to_all | solution.py:255
  387.2 371.1 %all-reduce.25.cloned.1.call-start = ((), (), s32[]{:S(2)}) async-start(), calls=%async_computation.16 | async-start | bytes 28311552 | tf_op jit(solution)/shard_map/psum | solution.py:277
  424.3 482.2 %reduce-scatter.7.cloned.1.call-start = ((), (), s32[]{:S(2)}) async-start(), calls=%async_computation.12 | async-start | bytes 2506752 | tf_op jit(solution)/shard_map/reduce_scatter | solution.py:293
  761.2 159.2 %reduce-scatter.13.cloned.1.call-start = ((), (), s32[]{:S(2)}) async-start(), calls=%async_computation.15 | async-start | bytes 7520256
  767.2 268.8 %reduce-scatter.9.cloned.1.call-start = ((), (), s32[]{:S(2)}) async-start(), calls=%async_computation.13 | async-start | bytes 10027008 | tf_op jit(solution)/shard_map/reduce_scatter | solution.py:294
  774.6 377.0 %reduce-scatter.11.cloned.1.call-start = ((), (), s32[]{:S(2)}) async-start(), calls=%async_computation.14 | async-start | bytes 10027008 | tf_op jit(solution)/shard_map/reduce_scatter | solution.py:295
  781.5 45.1 %copy-start.31 = (bf16[768]{0:T(1024)(128)(2,1)S(1)}, bf16[768]{0:T(1024)(128)(2,1)}, u32[]{:S(2)}) copy-start(bf16[768]{0:T(1024)(128)(2,1)} %get-tuple-element.580) | copy-start | bytes 4612
  781.6 45.1 %copy-start.32 = (bf16[768]{0:T(1024)(128)(2,1)S(1)}, bf16[768]{0:T(1024)(128)(2,1)}, u32[]{:S(2)}) copy-start(bf16[768]{0:T(1024)(128)(2,1)} %get-tuple-element.582) | copy-start | bytes 4612
  781.6 45.1 %copy-start.33 = (bf16[768]{0:T(1024)(128)(2,1)S(1)}, bf16[768]{0:T(1024)(128)(2,1)}, u32[]{:S(2)}) copy-start(bf16[768]{0:T(1024)(128)(2,1)} %get-tuple-element.664) | copy-start | bytes 4612
  781.6 45.1 %copy-start.34 = (bf16[768]{0:T(1024)(128)(2,1)S(1)}, bf16[768]{0:T(1024)(128)(2,1)}, u32[]{:S(2)}) copy-start(bf16[768]{0:T(1024)(128)(2,1)} %get-tuple-element.668) | copy-start | bytes 4612
  781.6 45.1 %copy-start.35 = (bf16[3072]{0:T(1024)(128)(2,1)S(1)}, bf16[3072]{0:T(1024)(128)(2,1)}, u32[]{:S(2)}) copy-start(bf16[3072]{0:T(1024)(128)(2,1)} %get-tuple-element.666) | copy-start | bytes 18436
  781.6 45.1 %copy-start.45 = (bf16[768]{0:T(1024)(128)(2,1)S(1)}, bf16[768]{0:T(1024)(128)(2,1)}, u32[]{:S(2)}) copy-start(bf16[768]{0:T(1024)(128)(2,1)} %get-tuple-element.569) | copy-start | bytes 4612
  781.6 45.1 %copy-start.46 = (bf16[768]{0:T(1024)(128)(2,1)S(1)}, bf16[768]{0:T(1024)(128)(2,1)}, u32[]{:S(2)}) copy-start(bf16[768]{0:T(1024)(128)(2,1)} %get-tuple-element.575) | copy-start | bytes 4612
  781.6 119.2 %copy-start.28 = (f32[512]{0:T(512)S(1)}, f32[512]{0:T(512)}, u32[]{:S(2)}) copy-start(f32[512]{0:T(512)} %copy-done.27) | copy-start | bytes 6148
  (45 other events, 403.9 us)
Sparse Core Ops, SparseCore 0:
  10.3 50.2 all-gather.4
  62.8 36.8 all-gather.6
  102.0 51.9 all-gather.8
  156.1 51.7 all-gather.10
  424.4 333.8 all-reduce.24
  762.5 63.8 reduce-scatter.6
  831.0 89.3 reduce-scatter.12
  925.1 110.9 reduce-scatter.8
  1040.7 110.8 reduce-scatter.10
where the time goes:
time: 1170 us; the launch traced here: 1160 us
  waiting for transfers between devices  627 us (54%)
  blocking collectives  173 us (15%)
  matrix products  142 us (12%)
  local copies, waits for them, and re-layouts  115 us (10%)
  other arithmetic  66 us (6%)
  between operations  19 us (2%)
  starting transfers between devices  16.5 us (1%)
    psum x1, waiting for transfers between devices, body(): lax.psum(grad_w_qkv.astype(jnp.bfloat16), 'seq').astype(jnp.float32)  334 us
    unnamed x2, blocking collectives  124 us
    reduce_scatter x1, waiting for transfers between devices, body(): lax.psum_scatter(pair_in, 'fsdp', scatter_dimension=0, tiled=True)  116 us
    reduce_scatter x1, waiting for transfers between devices, body(): lax.psum_scatter(pair_back, 'fsdp', scatter_dimension=0, tiled=True)  116 us
    psum x1, blocking collectives, body(): lax.psum((jnp.sum(valid_rows * tokens_f * tokens_f), jnp.sum(valid_rows *...  40.3 us
    dot_general x4, matrix products, block_scores(): jnp.einsum('qhd,khd->hqk', query_blk, key_pos, preferred_element_type=jnp...  33.6 us
    unnamed x132, local copies, waits for them, and re-layouts  24.9 us
  transfers between devices with their start and end apart: 13, of which 8 were waited for; matrix products, arithmetic and copies ran while one was open for 15% of the time, Pallas kernels for 0%

commit v1 on v0

--- a/solution.py
+++ b/solution.py
@@ -7,6 +7,10 @@
 HD = 64
 eps_norm = 1e-05
 masked_fill = -1e30
+
+
+def place_outputs_now(x_in, device_axis):
+    return jnp.sum(lax.all_gather(x_in, axis_name=device_axis), 0)
 
 
 def layer_norm(values, gain, shift):
@@ -274,7 +278,7 @@
         pair_gain_two,
         pair_shift_two,
     ) = (
-        lax.psum(grad_w_qkv.astype(jnp.bfloat16), "seq").astype(jnp.float32),
+        place_outputs_now(grad_w_qkv.astype(jnp.bfloat16), "seq").astype(jnp.float32),
         lax.psum(grad_w_out.astype(jnp.bfloat16), "seq").astype(jnp.float32),
         lax.psum(grad_w_in.astype(jnp.bfloat16), "seq").astype(jnp.float32),
         lax.psum(grad_w_back.astype(jnp.bfloat16), "seq").astype(jnp.float32),

time: 1170 us -> 1080 us (0.923)
  waiting for transfers between devices: 627 us -> 399 us
  other arithmetic: 66 us -> 144 us
  blocking collectives: 173 us -> 222 us
  local copies, waits for them, and re-layouts: 115 us -> 131 us
    psum x1, waiting for transfers between devices: 334 us -> 103 us  [body(): lax.psum(grad_w_out.astype(jnp.bfloat16), 'seq').astype(jnp.float32)]
    all_gather x0 -> x1, waiting for transfers between devices: none -> 87.7 us  [place_outputs_now(): return jnp.sum(lax.all_gather(x_in, axis_name=device_axis), 0)]
    reduce_sum x0 -> x1, other arithmetic: none -> 74.5 us  [place_outputs_now(): return jnp.sum(lax.all_gather(x_in, axis_name=device_axis), 0)]
    reduce_scatter x1, waiting for transfers between devices: 116 us -> 65.6 us  [body(): lax.psum_scatter(pair_in, 'fsdp', scatter_dimension=0, tiled=True)]
    all_to_all x0 -> x1, blocking collectives: none -> 48.9 us  [body(): lax.all_to_all(d_joint_stored, 'seq', split_axis=0, concat_axis=2, tiled=...]
    all_gather x0 -> x1, local copies, waits for them, and re-layouts: none -> 15.2 us  [place_outputs_now(): return jnp.sum(lax.all_gather(x_in, axis_name=device_axis), 0)]
    unnamed x10 -> x11, waiting for transfers between devices: 16.6 us -> 2.68 us
    all_to_all x1 -> x0, waiting for transfers between devices: 13.4 us -> none  [body(): lax.all_to_all(d_joint_stored, 'seq', split_axis=0, concat_axis=2, tiled=...]
  transfers between devices with their start and end apart: 13 -> 13, of which waited for: 8 -> 6; matrix products, arithmetic and copies ran while one was open for 15% -> 36% of each run, Pallas kernels for 0% -> 0%
where the time goes in v1:
time: 1080 us; the launch traced here: 1070 us
  waiting for transfers between devices  399 us (37%)
  blocking collectives  222 us (21%)
  matrix products  147 us (14%)
  other arithmetic  144 us (13%)
  local copies, waits for them, and re-layouts  131 us (12%)
  between operations  19.4 us (2%)
  starting transfers between devices  12.9 us (1%)
    unnamed x2, blocking collectives  122 us
    reduce_scatter x1, waiting for transfers between devices, body(): lax.psum_scatter(pair_back, 'fsdp', scatter_dimension=0, tiled=True)  115 us
    psum x1, waiting for transfers between devices, body(): lax.psum(grad_w_out.astype(jnp.bfloat16), 'seq').astype(jnp.float32)  103 us
    all_gather x1, waiting for transfers between devices, place_outputs_now(): return jnp.sum(lax.all_gather(x_in, axis_name=device_axis), 0)  87.7 us
    reduce_sum x1, other arithmetic, place_outputs_now(): return jnp.sum(lax.all_gather(x_in, axis_name=device_axis), 0)  74.5 us
    reduce_scatter x1, waiting for transfers between devices, body(): lax.psum_scatter(pair_in, 'fsdp', scatter_dimension=0, tiled=True)  65.6 us
    all_to_all x1, blocking collectives, body(): lax.all_to_all(d_joint_stored, 'seq', split_axis=0, concat_axis=2, tiled=...  48.9 us
    psum x1, blocking collectives, body(): lax.psum((jnp.sum(valid_rows * tokens_f * tokens_f), jnp.sum(valid_rows *...  41.7 us
  transfers between devices with their start and end apart: 13, of which 6 were waited for; matrix products, arithmetic and copies ran while one was open for 36% of the time, Pallas kernels for 0%

profile of v1, /device:TPU:0, one launch (start us, length us, event | category | flops | bytes accessed | tf_op | source)
XLA Modules:
  0.0 1074.9 jit_solution(13788863984707627514)
XLA Ops:
  19.6 63.9 %all-reduce.20 = (bf16[768]{0:T(1024)(128)(2,1)S(1)}, bf16[768]{0:T(1024)(128)(2,1)S(1)}, bf16[768]{0:T(1024)(128)(2,1)}, bf16[768]{0:T(1024)(128)(2,1)}, bf16[7...) all-reduce(bf16[768]{0:T(1024)(128)(2,1)S(1)} %dynamic-update-slice, ...), channel_id=1, replica_groups=mesh['seq'=2,'fsdp'=16] {'fsdp'}, use_global_device_ids=true, to_apply=%add.1 | all-reduce | flops 9216 | bytes 36864
  105.5 17.5 %all-to-all-done = bf16[512,3,2,384]{3,0,1,2:T(8,128)(2,1)S(1)} async-done(((bf16[512,3,2,384]{3,0,1,2:T(8,128)(2,1)}), bf16[512,3,2,384]{3,0,1,2:T(8,128)(2,1)S(1)}, u32[]{:S(2)}, u32[]{:S(2)}) %all-to-all-start) | async-done | bytes 2359328 | tf_op jit(solution)/shard_map/all_to_all | solution.py:88
  155.7 31.1 %while.38 = (s32[]{:T(128)}, bf16[6,1024,1024]{2,1,0:T(8,128)(2,1)}, bf16[1024,6,64]{0,2,1:T(8,128)(2,1)S(1)}, f32[6,1024,1]{1,0,2:T(8,128)S(1)}, bf16[1024,6,64...) while((s32[]{:T(128)}, ...), condition=%wide.region_4.5_spmd.clone, body=%wide.region_1.4_spmd.clone.sunk | while | flops 846395392 | bytes 65397944 | solution.py:131
  219.9 20.9 %multiply_convert_fusion.1 = (bf16[512,3072]{1,0:T(8,128)(2,1)}, f32[512,3072]{1,0:T(8,128)}, f32[512,3072]{1,0:T(8,128)}) fusion(f32[3072]{0:T(1024)S(1)} %convert_element_type.219, bf16[768,3072]{1,0:T(8,128)(2,1)} %all-gather.11.cloned.1.call-done, f32[512,768]{1,0:T(8,128)} %copy-done.4, f32[768]{0:T(1024)S(1)} %convert_element_type.217, ...), kind=kOutput, calls=%fused_computation.47 | convolution fusion | flops 2521694208 | bytes 22042624 | tf_op jit(solution)/shard_map/dot_general | solution.py:164
  252.8 10.0 fusion.61
  304.6 66.7 %while.39 = (s32[]{:T(128)}, bf16[6,1024,1024]{2,1,0:T(8,128)(2,1)}, bf16[1024,6,64]{0,2,1:T(8,128)(2,1)}, f32[1024,6,64]{0,2,1:T(8,128)S(1)}, f32[1024,6,64]{0,...) while((s32[]{:T(128)}, ...), condition=%wide.region_15.16_spmd.clone, body=%wide.region_13.0_spmd.clone.sunk | while | flops 2050029568 | bytes 127470920 | solution.py:239
  308.4 9.4 multiply_reduce_fusion.6
  317.8 7.4 bitcast_add_fusion.5
  325.3 9.1 constant_dynamic-update-slice_fusion.2
  341.9 9.5 multiply_reduce_fusion.6
  351.4 7.4 bitcast_add_fusion.5
  358.8 9.0 constant_dynamic-update-slice_fusion.2
  386.0 8.3 pad_maximum_fusion
  400.8 48.9 %all_to_all.60 = bf16[1024,3,1,384]{3,1,2,0:T(4,128)(2,1)S(1)} all-to-all(bf16[1024,3,1,384]{3,1,2,0:T(4,128)(2,1)S(1)} %bitcast.151), channel_id=1, replica_groups=mesh['seq'=2,'fsdp'=16] {'seq'}, dimensions={0} | all-to-all | bytes 4718592 | tf_op jit(solution)/shard_map/all_to_all | solution.py:259
  458.0 103.3 %all-reduce.25.cloned.1.call-done = (bf16[768,768]{1,0:T(8,128)(2,1)}, bf16[768,3072]{1,0:T(8,128)(2,1)}, bf16[3072,768]{1,0:T(8,128)(2,1)}) async-done(((bf16[768,768]{1,0:T(8,128)(2,1)}, bf16[768,3072]{1,0:T(8,128)(2,1)}, bf16[3072,768]{1,0:T(8,128)(2,1)}), (bf16[768,768]{1,0:T(8,128)(2,1)}, bf16[768,3072]{1,0:T(8,128)(2,1)}, bf16[3072,768]{1,0:T(8,128)(2,1)})) %all-reduce.25.cloned.1.call-update) | async-done | bytes 10616848 | tf_op jit(solution)/shard_map/psum | solution.py:282
  564.2 87.7 %all-gather.15.cloned.1.call-done = bf16[1536,2304]{0,1:T(8,128)(2,1)} async-done(((bf16[768,2304]{0,1:T(8,128)(2,1)}), bf16[1536,2304]{0,1:T(8,128)(2,1)}) %all-gather.15.cloned.1.call-update) | async-done | bytes 7077904 | tf_op jit(solution)/shard_map/all_gather | solution.py:13
  651.9 15.2 %reshape.274 = bf16[2,768,2304]{1,0,2:T(2,128)(2,1)} reshape(bf16[1536,2304]{0,1:T(8,128)(2,1)} %all-gather.15.cloned.1.call-done) | data formatting | bytes 14155776 | tf_op jit(solution)/shard_map/all_gather | solution.py:13
  667.1 74.5 %reduce_sum.282 = bf16[768,2304]{0,1:T(8,128)(2,1)S(1)} reduce(bf16[2,768,2304]{1,0,2:T(2,128)(2,1)} %reshape.274, bf16[]{:T(256)} %constant.166.clone.1), dimensions={0}, to_apply=%region_16.17 | reduce | flops 1769472 | bytes 10616834 | tf_op jit(solution)/shard_map/reduce_sum | solution.py:13
  754.1 7.5 convert_element_type.242
  763.3 41.7 %all-reduce.18 = (f32[1]{0:T(128)}, f32[1]{0:T(128)}, f32[1]{0:T(128)}, f32[]{:T(128)}) all-reduce(f32[1]{0:T(128)} %bitcast.38, f32[1]{0:T(128)} %bitcast.37, f32[1]{0:T(128)} %bitcast.36, f32[]{:T(128)} %get-tuple-element.625), channel_id=1, replica_groups=mesh['seq'=2,'fsdp'=16] {'seq','fsdp'}, use_global_device_ids=true, to_apply=%region_56.57 | all-reduce | flops 4 | bytes 32 | tf_op jit(solution)/shard_map/psum | solution.py:178
  808.5 9.1 all-reduce.21
  817.7 58.5 %all-reduce.19 = (f32[768]{0:T(1024)S(1)}, f32[768]{0:T(1024)S(1)}, f32[768]{0:T(1024)S(1)}, f32[768]{0:T(1024)S(1)}, f32[768]{0:T(1024)S(1)}, /*index=5*/f32[30...) all-reduce(bf16[768]{0:T(1024)(128)(2,1)S(1)} %get-tuple-element.61, ...), channel_id=7, replica_groups=mesh['seq'=2,'fsdp'=16] {'fsdp'}, use_global_device_ids=true, to_apply=%region_26.27.clone | all-reduce | flops 9216 | bytes 55296
  886.9 65.6 %reduce-scatter.9.cloned.1.call-done = f32[48,3072]{1,0:T(8,128)} async-done(((f32[768,3072]{1,0:T(8,128)}), f32[48,3072]{1,0:T(8,128)}) %reduce-scatter.9.cloned.1.call-update) | async-done | bytes 589840 | tf_op jit(solution)/shard_map/reduce_scatter | solution.py:298
  952.5 115.4 %reduce-scatter.11.cloned.1.call-done = f32[192,768]{1,0:T(8,128)} async-done(((f32[3072,768]{1,0:T(8,128)}), f32[192,768]{1,0:T(8,128)}) %reduce-scatter.11.cloned.1.call-update) | async-done | bytes 589840 | tf_op jit(solution)/shard_map/reduce_scatter | solution.py:299
  (265 shorter events, 255.4 us)
Async XLA Ops:
  7.2 76.4 %all-gather.7.cloned.1.call-start = ((), (), s32[]{:S(2)}) async-start(), calls=%async_computation.8 | async-start | bytes 3760128 | tf_op jit(solution)/shard_map/all_gather | solution.py:62
  7.9 207.0 %all-gather.9.cloned.1.call-start = ((), (), s32[]{:S(2)}) async-start(), calls=%async_computation.9 | async-start | bytes 1253376 | tf_op jit(solution)/shard_map/all_gather | solution.py:63
  8.7 211.3 %all-gather.11.cloned.1.call-start = ((), (), s32[]{:S(2)}) async-start(), calls=%async_computation.10 | async-start | bytes 5013504 | tf_op jit(solution)/shard_map/all_gather | solution.py:157
  95.7 27.3 %all-to-all-start = ((bf16[512,3,2,384]{3,0,1,2:T(8,128)(2,1)}), bf16[512,3,2,384]{3,0,1,2:T(8,128)(2,1)S(1)}, u32[]{:S(2)}, u32[]{:S(2)}) async-start(bf16[512,3,2,384]{3,0,1,2:T(8,128)(2,1)} %copy.101), calls=%async_computation | async-start | bytes 4718592 | tf_op jit(solution)/shard_map/all_to_all | solution.py:88
  99.6 141.2 %all-gather.13.cloned.1.call-start = ((), (), s32[]{:S(2)}) async-start(), calls=%async_computation.11 | async-start | bytes 5013504 | tf_op jit(solution)/shard_map/all_gather | solution.py:158
  105.5 21.5 %copy-start.22 = (s32[1024]{0:T(1024)}, s32[1024]{0:T(1024)S(1)}, u32[]{:S(2)}) copy-start(s32[1024]{0:T(1024)S(1)} %fusion.50) | copy-start | bytes 12292
  155.7 32.4 %copy-start.20 = (s32[1024]{0:T(1024)S(1)}, s32[1024]{0:T(1024)}, u32[]{:S(2)}) copy-start(s32[1024]{0:T(1024)} %broadcast_clamp_fusion) | copy-start | bytes 12292
  194.8 12.9 %all-to-all-start.1 = ((bf16[2,2,98304]{2,1,0:T(2,128)(2,1)}), bf16[2,2,98304]{2,1,0:T(2,128)(2,1)}, u32[]{:S(2)}, u32[]{:S(2)}) async-start(bf16[2,2,98304]{2,1,0:T(2,128)(2,1)} %reshape.337), calls=%async_computation.1 | async-start | bytes 1572864 | tf_op jit(solution)/shard_map/all_to_all | solution.py:144
  276.5 12.6 %all-to-all-start.2 = ((bf16[512,2,384]{2,0,1:T(8,128)(2,1)}), bf16[512,2,384]{2,0,1:T(8,128)(2,1)S(1)}, u32[]{:S(2)}, u32[]{:S(2)}) async-start(bf16[512,2,384]{2,0,1:T(8,128)(2,1)} %bitcast.160), calls=%async_computation.2 | async-start | bytes 1572864 | tf_op jit(solution)/shard_map/all_to_all | solution.py:204
  280.1 281.2 %all-reduce.25.cloned.1.call-start = ((), (), s32[]{:S(2)}) async-start(), calls=%async_computation.17 | async-start | bytes 21233664 | tf_op jit(solution)/shard_map/psum | solution.py:282
  289.0 362.9 %all-gather.15.cloned.1.call-start = ((), (), s32[]{:S(2)}) async-start(), calls=%async_computation.15 | async-start | bytes 10616832 | tf_op jit(solution)/shard_map/all_gather | solution.py:13
  458.0 428.9 %reduce-scatter.7.cloned.1.call-start = ((), (), s32[]{:S(2)}) async-start(), calls=%async_computation.12 | async-start | bytes 2506752 | tf_op jit(solution)/shard_map/reduce_scatter | solution.py:297
  564.1 322.7 %reduce-scatter.13.cloned.1.call-start = ((), (), s32[]{:S(2)}) async-start(), calls=%async_computation.16 | async-start | bytes 7520256
  746.4 206.1 %reduce-scatter.9.cloned.1.call-start = ((), (), s32[]{:S(2)}) async-start(), calls=%async_computation.13 | async-start | bytes 10027008 | tf_op jit(solution)/shard_map/reduce_scatter | solution.py:298
  754.0 313.8 %reduce-scatter.11.cloned.1.call-start = ((), (), s32[]{:S(2)}) async-start(), calls=%async_computation.14 | async-start | bytes 10027008 | tf_op jit(solution)/shard_map/reduce_scatter | solution.py:299
  761.6 46.5 %copy-start.6 = (bf16[512,3,2,1,384]{0,4,2,1,3:T(8,128)(2,1)S(1)}, bf16[512,3,2,1,384]{0,4,2,1,3:T(8,128)(2,1)}, u32[]{:S(2)}) copy-start(bf16[512,3,2,1,384]{0,4,2,1,3:T(8,128)(2,1)} %copy.117) | copy-start | bytes 7077892
  761.6 46.8 %copy-start.28 = (bf16[768]{0:T(1024)(128)(2,1)S(1)}, bf16[768]{0:T(1024)(128)(2,1)}, u32[]{:S(2)}) copy-start(bf16[768]{0:T(1024)(128)(2,1)} %get-tuple-element.544) | copy-start | bytes 4612
  761.6 46.8 %copy-start.29 = (bf16[768]{0:T(1024)(128)(2,1)S(1)}, bf16[768]{0:T(1024)(128)(2,1)}, u32[]{:S(2)}) copy-start(bf16[768]{0:T(1024)(128)(2,1)} %get-tuple-element.546) | copy-start | bytes 4612
  761.6 46.8 %copy-start.30 = (bf16[768]{0:T(1024)(128)(2,1)S(1)}, bf16[768]{0:T(1024)(128)(2,1)}, u32[]{:S(2)}) copy-start(bf16[768]{0:T(1024)(128)(2,1)} %get-tuple-element.627) | copy-start | bytes 4612
  761.7 46.8 %copy-start.31 = (bf16[768]{0:T(1024)(128)(2,1)S(1)}, bf16[768]{0:T(1024)(128)(2,1)}, u32[]{:S(2)}) copy-start(bf16[768]{0:T(1024)(128)(2,1)} %get-tuple-element.631) | copy-start | bytes 4612
  761.7 46.8 %copy-start.32 = (bf16[3072]{0:T(1024)(128)(2,1)S(1)}, bf16[3072]{0:T(1024)(128)(2,1)}, u32[]{:S(2)}) copy-start(bf16[3072]{0:T(1024)(128)(2,1)} %get-tuple-element.629) | copy-start | bytes 18436
  761.7 46.8 %copy-start.40 = (bf16[768]{0:T(1024)(128)(2,1)S(1)}, bf16[768]{0:T(1024)(128)(2,1)}, u32[]{:S(2)}) copy-start(bf16[768]{0:T(1024)(128)(2,1)} %get-tuple-element.533) | copy-start | bytes 4612
  761.7 46.8 %copy-start.41 = (bf16[768]{0:T(1024)(128)(2,1)S(1)}, bf16[768]{0:T(1024)(128)(2,1)}, u32[]{:S(2)}) copy-start(bf16[768]{0:T(1024)(128)(2,1)} %get-tuple-element.539) | copy-start | bytes 4612
  761.7 119.7 %copy-start.27 = (f32[512]{0:T(512)S(1)}, f32[512]{0:T(512)}, u32[]{:S(2)}) copy-start(f32[512]{0:T(512)} %copy-done.26) | copy-start | bytes 6148
  (39 other events, 269.4 us)
Sparse Core Ops, SparseCore 0:
  10.3 50.2 all-gather.6
  62.8 36.8 all-gather.8
  102.0 51.9 all-gather.10
  156.1 51.7 all-gather.12
  289.1 272.0 all-reduce.24
  562.7 89.2 all-gather.14
  656.3 63.2 reduce-scatter.6
  746.5 90.4 reduce-scatter.12
  841.7 110.7 reduce-scatter.8
  957.0 110.8 reduce-scatter.10
